TPU v7x, 256 devices: a whole 4x4x8 slice. The times are simulated.
256 devices in a mesh: freq: 32 (over x, z_lo, core), mz: 8 (over y, z_hi).
Axes of the slice: x: 4, y: 4, z: 8 (z_hi: 2, z_lo: 4; z = z_hi * 4 + z_lo), core: 2. Of those that a mesh axis runs over, the one named last changes fastest.
Arguments:
- intensity: bfloat16 [8, 6144, 4096], P(None, 'freq', 'mz'), may hold values from -6 to 6
- elution: float32 [6144, 64], P(('freq', 'mz')), may hold values from -6 to 6
- loadings: float32 [8, 64], replicated, may hold values from 0.0005 to 0.01
- shifts: int32 [8, 64], replicated, may hold values from 0 to 255
- bin_weight: float32 [6144], replicated, may hold values from 0.25 to 4
Outputs:
- spectral: float32 [64, 4096], P(None, ('mz', 'freq'))
All inputs are finite; a program needn't handle non-finite values.
Results may differ from a plain program's by a relative error of at most 0.0003.
Values may be sent and summed in bfloat16 or wider, within the bound.
A program may use at most 64 MiB of HBM per device.

v0:
```python
import math
import jax
import jax.numpy as jnp
from jax import lax
from jax.sharding import PartitionSpec as P

PRECISE = lax.Precision.HIGHEST


def turn_angle(product, length):
    return 2.0 * math.pi / length * (product % length).astype(jnp.float32)


def cholesky_solve(gram_matrix, numerator):
    factor = jnp.linalg.cholesky(gram_matrix)
    middle = lax.linalg.triangular_solve(factor, numerator, left_side=True, lower=True)
    return lax.linalg.triangular_solve(factor, middle, left_side=True, lower=True, transpose_a=True)


def on_device(intensity, elution, loadings, shifts, bin_weight):
    freq_count = lax.axis_size("freq")
    mz_count = lax.axis_size("mz")
    freq_rank = lax.axis_index("freq")
    mz_rank = lax.axis_index("mz")
    run_count, bin_count, local_mz = intensity.shape
    length = bin_count * freq_count
    components = loadings.shape[1]
    block_len = bin_count // freq_count
    norm_scale = 1.0 / math.sqrt(length)
    dev_ids = jnp.arange(freq_count, dtype=jnp.int32)
    bin_ids = jnp.arange(bin_count, dtype=jnp.int32)
    dev_angle = turn_angle(dev_ids[:, None] * dev_ids[None, :], freq_count)
    cos_dev = jnp.cos(dev_angle)
    sin_dev = jnp.sin(dev_angle)
    my_times = freq_rank * block_len + jnp.arange(block_len, dtype=jnp.int32)
    twiddle = turn_angle(dev_ids[:, None] * my_times[None, :], length)
    twid_cos = jnp.cos(twiddle)[None, :, :, None]
    twid_sin = jnp.sin(twiddle)[None, :, :, None]
    bin_angle = turn_angle(bin_ids[:, None] * bin_ids[None, :], bin_count)
    cos_bin = jnp.cos(bin_angle)
    sin_bin = jnp.sin(bin_angle)
    full_elution = lax.all_gather(elution, ("freq", "mz"), axis=0, tiled=True)
    stacked = full_elution.reshape(freq_count, bin_count, components)
    weights_grid = bin_weight.reshape(bin_count, freq_count)
    weights_mine = lax.dynamic_slice_in_dim(weights_grid, freq_rank, 1, 1)[:, 0]
    bins_mine = freq_rank + freq_count * bin_ids
    row_angle = turn_angle(freq_rank * dev_ids, freq_count)
    part_re = jnp.einsum("p,pqr->qr", jnp.cos(row_angle), stacked, precision=PRECISE)
    part_im = -jnp.einsum("p,pqr->qr", jnp.sin(row_angle), stacked, precision=PRECISE)
    own_twid = turn_angle(freq_rank * bin_ids, length)[:, None]
    turn_re = part_re * jnp.cos(own_twid) + part_im * jnp.sin(own_twid)
    turn_im = part_im * jnp.cos(own_twid) - part_re * jnp.sin(own_twid)
    own_re = (
        jnp.dot(cos_bin, turn_re, precision=PRECISE) + jnp.dot(sin_bin, turn_im, precision=PRECISE)
    ) * norm_scale
    own_im = (
        jnp.dot(cos_bin, turn_im, precision=PRECISE) - jnp.dot(sin_bin, turn_re, precision=PRECISE)
    ) * norm_scale
    weights_col = weights_mine[None, :, None]

    def own_model(run_amp, run_lag):
        phase = turn_angle(bins_mine[None, :, None] * run_lag[:, None, :], length)
        phase_cos = jnp.cos(phase)
        phase_sin = jnp.sin(phase)
        model_re = run_amp[:, None, :] * (own_re * phase_cos + own_im * phase_sin)
        model_im = run_amp[:, None, :] * (own_im * phase_cos - own_re * phase_sin)
        return (model_re, model_im)

    samples = lax.all_to_all(
        intensity.reshape(run_count, 1, bin_count, local_mz),
        "freq",
        split_axis=2,
        concat_axis=1,
        tiled=True,
    ).astype(jnp.float32)
    raw_re = jnp.einsum("ap,kpim->kaim", cos_dev, samples, precision=PRECISE)
    raw_im = -jnp.einsum("ap,kpim->kaim", sin_dev, samples, precision=PRECISE)
    half_re = raw_re * twid_cos + raw_im * twid_sin
    half_im = raw_im * twid_cos - raw_re * twid_sin
    half_re, half_im = (half_re, half_im)
    piece_re = lax.all_to_all(half_re, "freq", split_axis=1, concat_axis=2, tiled=True)[:, 0]
    piece_im = lax.all_to_all(half_im, "freq", split_axis=1, concat_axis=2, tiled=True)[:, 0]
    out_re = jnp.einsum("bq,kqm->kbm", cos_bin, piece_re, precision=PRECISE) + jnp.einsum(
        "bq,kqm->kbm", sin_bin, piece_im, precision=PRECISE
    )
    out_im = jnp.einsum("bq,kqm->kbm", cos_bin, piece_im, precision=PRECISE) - jnp.einsum(
        "bq,kqm->kbm", sin_bin, piece_re, precision=PRECISE
    )
    model_re, model_im = own_model(loadings, shifts)
    numerator = (
        jnp.einsum("kbr,kbm->rm", weights_col * model_re, out_re, precision=PRECISE)
        + jnp.einsum("kbr,kbm->rm", weights_col * model_im, out_im, precision=PRECISE)
    ) * norm_scale
    run_share = run_count // mz_count
    run_amp = lax.dynamic_slice_in_dim(loadings, mz_rank * run_share, run_share, 0)
    run_lag = lax.dynamic_slice_in_dim(shifts, mz_rank * run_share, run_share, 0)
    model_re, model_im = own_model(run_amp, run_lag)
    gram_matrix = lax.psum(
        jnp.einsum("kbr,kbs->rs", weights_col * model_re, model_re, precision=PRECISE)
        + jnp.einsum("kbr,kbs->rs", weights_col * model_im, model_im, precision=PRECISE),
        ("freq", "mz"),
    )
    owned = lax.psum_scatter(numerator, "freq", scatter_dimension=1, tiled=True)
    return cholesky_solve(gram_matrix, owned)


def solution(mesh):
    in_specs = (P(None, "freq", "mz"), P(("freq", "mz"), None), P(), P(), P())
    out_specs = P(None, ("mz", "freq"))
    return jax.shard_map(
        on_device, mesh=mesh, in_specs=in_specs, out_specs=out_specs, check_vma=False
    )
```

profile of v0, /device:TPU:8, one launch (start us, length us, event | category | flops | bytes accessed | tf_op | source)
XLA Modules:
  0.0 1164.9 jit_solution(4711913364988517103)
XLA Ops:
  6.5 3.4 copy.76
  10.0 8.7 all-to-all-start
  18.7 0.1 fusion.179
  18.9 38.9 %all-to-all-done = bf16[8,1,192,512]{3,0,1,2:T(8,128)(2,1)S(1)} async-done(((bf16[8,1,192,512]{3,0,1,2:T(8,128)(2,1)}), bf16[8,1,192,512]{3,0,1,2:T(8,128)(2,1)S(1)}, u32[]{:S(2)}, u32[]{:S(2)}) %all-to-all-start) | async-done | bytes 1572896 | tf_op jit(solution)/shard_map/all_to_all | solution.py:69
  57.8 3.0 fusion.14
  60.8 5.3 subtract_bitcast_fusion
  66.1 3.5 copy.42
  69.6 4.3 all-to-all-start.1
  73.9 5.4 copy.44
  79.2 67.4 %all-to-all-done.1 = f32[8,32,6,512]{3,0,2,1:T(8,128)S(1)} async-done(((f32[8,32,6,512]{3,0,2,1:T(8,128)}), f32[8,32,6,512]{3,0,2,1:T(8,128)S(1)}, u32[]{:S(2)}, u32[]{:S(2)}) %all-to-all-start.1) | async-done | bytes 3145760 | tf_op jit(solution)/shard_map/all_to_all | solution.py:81
  146.7 4.8 all-to-all-start.2
  151.5 0.0 all-gather.2.cloned.1.call-start
  151.5 0.7 all-gather.2.cloned.1.call-update
  152.2 0.0 reduce-scatter.4.cloned.1.call-start
  152.3 0.0 copy-done.2
  152.3 0.1 reshape.152
  152.4 0.2 dynamic-slice_reduce_fusion
  152.5 0.0 copy-done.4
  152.6 0.0 copy-done.3
  152.6 0.1 fusion.204
  152.7 0.1 fusion.202
  152.7 692.2 %all-gather.2.cloned.1.call-done = f32[6144,64]{1,0:T(8,128)} async-done(((f32[24,64]{1,0:T(8,128)}), f32[6144,64]{1,0:T(8,128)}) %all-gather.2.cloned.1.call-update) | async-done | bytes 1572880 | tf_op jit(solution)/shard_map/all_gather | solution.py:42
  844.9 2.6 multiply_reduce_fusion
  847.6 1.1 fusion.88
  848.7 1.1 fusion.86
  849.8 1.1 fusion.33
  850.9 1.1 fusion.34
  852.0 0.8 fusion.96
  852.8 0.8 convolution_add_fusion.1
  853.6 105.6 %psum.7 = f32[64,64]{0,1:T(8,128)S(1)} all-reduce(f32[64,64]{0,1:T(8,128)S(1)} %convolution_add_fusion.1), channel_id=1, replica_groups=mesh['freq'=32,'mz'=8] {'freq','mz'}, use_global_device_ids=true, to_apply=%region_0.1 | all-reduce | flops 4096 | bytes 32768 | tf_op jit(solution)/shard_map/psum | solution.py:98
  959.2 0.1 copy.38
  959.3 5.8 cholesky.16
  965.2 7.3 fusion.12
  972.5 7.4 fusion.10
  980.0 0.0 all-to-all-done.2
  980.0 7.5 fusion.8
  987.5 7.7 fusion.6
  995.1 0.0 copy-done.1
  995.1 0.0 copy-start
  995.2 8.6 fusion.18
  1003.8 9.4 fusion.30
  1013.2 0.0 reduce-scatter.4.cloned.1.call-update
  1013.2 0.6 compare_reduce_fusion
  1013.9 0.7 fusion.141
  1014.5 4.9 custom-call.8
  1019.4 136.5 %reduce-scatter.4.cloned.1.call-done = f32[16,64]{1,0:T(8,128)} async-done(((f32[512,64]{1,0:T(8,128)}), f32[16,64]{1,0:T(8,128)}) %reduce-scatter.4.cloned.1.call-update) | async-done | bytes 4112
  1156.0 0.8 fusion.144
  1156.8 0.8 fusion.142
  (11 shorter events, 0.1 us)
Async XLA Ops:
  10.0 47.8 %all-to-all-start = ((bf16[8,1,192,512]{3,0,1,2:T(8,128)(2,1)}), bf16[8,1,192,512]{3,0,1,2:T(8,128)(2,1)S(1)}, u32[]{:S(2)}, u32[]{:S(2)}) async-start(bf16[8,1,192,512]{3,0,1,2:T(8,128)(2,1)} %bitcast.79), calls=%async_computation | async-start | bytes 3145728 | tf_op jit(solution)/shard_map/all_to_all | solution.py:69
  69.6 77.1 %all-to-all-start.1 = ((f32[8,32,6,512]{3,0,2,1:T(8,128)}), f32[8,32,6,512]{3,0,2,1:T(8,128)S(1)}, u32[]{:S(2)}, u32[]{:S(2)}) async-start(f32[8,32,6,512]{3,0,2,1:T(8,128)} %copy.42), calls=%async_computation.1 | async-start | bytes 6291456 | tf_op jit(solution)/shard_map/all_to_all | solution.py:81
  79.2 73.0 %copy-start.2 = (f32[6144]{0:T(1024)S(1)}, f32[6144]{0:T(1024)}, u32[]{:S(2)}) copy-start(f32[6144]{0:T(1024)} %param.9) | copy-start | bytes 73732
  79.2 73.3 %copy-start.4 = (f32[8,64]{1,0:T(8,128)S(1)}, f32[8,64]{1,0:T(8,128)}, u32[]{:S(2)}) copy-start(f32[8,64]{1,0:T(8,128)} %param.7) | copy-start | bytes 6148
  79.2 73.4 %copy-start.3 = (s32[8,64]{1,0:T(8,128)S(1)}, s32[8,64]{1,0:T(8,128)}, u32[]{:S(2)}) copy-start(s32[8,64]{1,0:T(8,128)} %param.8) | copy-start | bytes 6148
  146.7 833.3 %all-to-all-start.2 = ((f32[8,32,6,512]{3,0,2,1:T(8,128)}), f32[8,32,6,512]{3,0,2,1:T(8,128)}, u32[]{:S(2)}, u32[]{:S(2)}) async-start(f32[8,32,6,512]{3,0,2,1:T(8,128)} %copy.44), calls=%async_computation.2 | async-start | bytes 6291456 | tf_op jit(solution)/shard_map/all_to_all | solution.py:82
  151.5 693.4 %all-gather.2.cloned.1.call-start = ((), (), s32[]{:S(2)}) async-start(), calls=%async_computation.4 | async-start | bytes 3158016 | tf_op jit(solution)/shard_map/all_gather | solution.py:42
  152.2 1003.7 %reduce-scatter.4.cloned.1.call-start = ((), (), s32[]{:S(2)}) async-start(), calls=%async_computation.5 | async-start | bytes 270336
  987.5 7.7 copy-start.1
  995.1 8.7 copy-start
Sparse Core Ops, SparseCore 0:
  154.2 690.7 all-gather.1
  1013.4 142.5 reduce-scatter.3
where the time goes:
time: 1170 us; the launch traced here: 1160 us
  waiting for transfers between devices  936 us (80%)
  blocking collectives  106 us (9%)
  matrix products  63.8 us (5%)
  starting transfers between devices  17.9 us (2%)
  other arithmetic  14.9 us (1%)
  between operations  14.1 us (1%)
  local copies, waits for them, and re-layouts  12.7 us (1%)
    all_gather x1, waiting for transfers between devices, on_device(): full_elution = lax.all_gather(elution, ('freq', 'mz'), axis=0, tiled=True)  692 us
    unnamed x3, waiting for transfers between devices  137 us
    psum x1, blocking collectives, on_device(): lax.psum(jnp.einsum('kbr,kbs->rs', weights_col * model_re, model_re, prec...  106 us
    all_to_all x1, waiting for transfers between devices, on_device(): lax.all_to_all(half_re, 'freq', split_axis=1, concat_axis=2, tiled=True)  67.4 us
    all_to_all x1, waiting for transfers between devices, on_device(): lax.all_to_all(intensity.reshape(run_count, 1, bin_count, local_mz), 'fre...  38.9 us
  transfers between devices with their start and end apart: 5, of which 4 were waited for; matrix products, arithmetic and copies ran while one was open for 4% of the time, Pallas kernels for 0%

commit v1 on v0

--- a/solution.py
+++ b/solution.py
@@ -78,7 +78,10 @@
     half_re = raw_re * twid_cos + raw_im * twid_sin
     half_im = raw_im * twid_cos - raw_re * twid_sin
     half_re, half_im = (half_re, half_im)
-    piece_re = lax.all_to_all(half_re, "freq", split_axis=1, concat_axis=2, tiled=True)[:, 0]
+    piece_re = jnp.concatenate(
+        lax.all_to_all(jnp.stack(jnp.split(half_re, lax.axis_size("freq"), axis=1)), "freq", 0, 0),
+        axis=2,
+    )[:, 0]
     piece_im = lax.all_to_all(half_im, "freq", split_axis=1, concat_axis=2, tiled=True)[:, 0]
     out_re = jnp.einsum("bq,kqm->kbm", cos_bin, piece_re, precision=PRECISE) + jnp.einsum(
         "bq,kqm->kbm", sin_bin, piece_im, precision=PRECISE

time: 1170 us -> 1190 us (1.017)
  local copies, waits for them, and re-layouts: 12.7 us -> 36.6 us
    unnamed x11 -> x44, local copies, waits for them, and re-layouts: 3.45 us -> 27.7 us
where the time goes in v1:
time: 1190 us; the launch traced here: 1180 us
  waiting for transfers between devices  935 us (79%)
  blocking collectives  106 us (9%)
  matrix products  60.1 us (5%)
  local copies, waits for them, and re-layouts  36.6 us (3%)
  starting transfers between devices  17.2 us (1%)
  other arithmetic  14.9 us (1%)
  between operations  14.1 us (1%)
    all_gather x1, waiting for transfers between devices, on_device(): full_elution = lax.all_gather(elution, ('freq', 'mz'), axis=0, tiled=True)  692 us
    unnamed x3, waiting for transfers between devices  137 us
    psum x1, blocking collectives, on_device(): lax.psum(jnp.einsum('kbr,kbs->rs', weights_col * model_re, model_re, prec...  106 us
    all_to_all x1, waiting for transfers between devices, on_device(): lax.all_to_all(jnp.stack(jnp.split(half_re, lax.axis_size('freq'), axis=1...  67.4 us
    all_to_all x1, waiting for transfers between devices, on_device(): lax.all_to_all(intensity.reshape(run_count, 1, bin_count, local_mz), 'fre...  38.9 us
    unnamed x44, local copies, waits for them, and re-layouts  27.7 us
  transfers between devices with their start and end apart: 5, of which 4 were waited for; matrix products, arithmetic and copies ran while one was open for 4% of the time, Pallas kernels for 0%

profile of v1, /device:TPU:8, one launch (start us, length us, event | category | flops | bytes accessed | tf_op | source)
XLA Modules:
  0.0 1183.8 jit_solution(16514409751802009263)
XLA Ops:
  6.5 3.4 copy.75
  10.0 8.7 all-to-all-start
  18.9 38.9 %all-to-all-done = bf16[8,1,192,512]{3,0,1,2:T(8,128)(2,1)S(1)} async-done(((bf16[8,1,192,512]{3,0,1,2:T(8,128)(2,1)}), bf16[8,1,192,512]{3,0,1,2:T(8,128)(2,1)S(1)}, u32[]{:S(2)}, u32[]{:S(2)}) %all-to-all-start) | async-done | bytes 1572896 | tf_op jit(solution)/shard_map/all_to_all | solution.py:69
  57.8 3.0 fusion.14
  60.8 5.3 subtract_bitcast_fusion
  66.7 0.7 fusion.125
  68.2 0.7 fusion.123
  68.9 0.7 fusion.122
  69.7 0.7 fusion.121
  70.4 0.7 fusion.120
  72.6 0.7 fusion.117
  73.3 0.7 fusion.116
  74.0 0.7 fusion.115
  75.5 0.7 fusion.113
  78.4 0.7 fusion.109
  79.8 0.7 fusion.107
  80.6 0.7 fusion.106
  81.3 0.7 fusion.105
  84.9 0.7 fusion.100
  85.7 0.7 fusion.99
  87.1 0.7 fusion.97
  87.9 0.7 fusion.96
  89.3 4.3 all-to-all-start.1
  93.6 5.4 copy.43
  99.0 67.4 %all-to-all-done.1 = f32[32,8,1,6,512]{4,2,3,1,0:T(1,128)S(1)} async-done(((f32[32,8,1,6,512]{4,2,3,1,0:T(1,128)}), f32[32,8,1,6,512]{4,2,3,1,0:T(1,128)S(1)}, u32[]{:S(2)}, u32[]{:S(2)}) %all-to-all-start.1) | async-done | bytes 3145760 | tf_op jit(solution)/shard_map/all_to_all | solution.py:82
  166.4 1.6 copy-done
  168.1 4.1 all-to-all-start.2
  173.4 691.6 %all-gather.2.cloned.1.call-done = f32[6144,64]{1,0:T(8,128)} async-done(((f32[24,64]{1,0:T(8,128)}), f32[6144,64]{1,0:T(8,128)}) %all-gather.2.cloned.1.call-update) | async-done | bytes 1572880 | tf_op jit(solution)/shard_map/all_gather | solution.py:42
  865.0 2.6 multiply_reduce_fusion
  867.7 1.1 fusion.88
  868.8 1.1 fusion.86
  869.9 1.1 fusion.33
  871.0 1.1 fusion.34
  872.1 0.8 fusion.128
  872.9 0.8 convolution_add_fusion.1
  873.7 105.7 %psum.7 = f32[64,64]{0,1:T(8,128)S(1)} all-reduce(f32[64,64]{0,1:T(8,128)S(1)} %convolution_add_fusion.1), channel_id=1, replica_groups=mesh['freq'=32,'mz'=8] {'freq','mz'}, use_global_device_ids=true, to_apply=%region_0.1 | all-reduce | flops 4096 | bytes 32768 | tf_op jit(solution)/shard_map/psum | solution.py:101
  979.5 5.8 cholesky.16
  985.3 2.5 copy.41
  987.8 7.3 fusion.12
  995.1 7.5 fusion.10
  1002.6 5.7 fusion.8
  1008.3 5.9 fusion.6
  1014.3 8.4 fusion.18
  1022.7 9.4 fusion.30
  1033.4 4.9 custom-call.8
  1038.3 136.6 %reduce-scatter.4.cloned.1.call-done = f32[16,64]{1,0:T(8,128)} async-done(((f32[512,64]{1,0:T(8,128)}), f32[16,64]{1,0:T(8,128)}) %reduce-scatter.4.cloned.1.call-update) | async-done | bytes 4112
  1174.9 0.8 fusion.176
  1175.8 0.8 fusion.174
  (45 shorter events, 13.5 us)
Async XLA Ops:
  10.0 47.8 %all-to-all-start = ((bf16[8,1,192,512]{3,0,1,2:T(8,128)(2,1)}), bf16[8,1,192,512]{3,0,1,2:T(8,128)(2,1)S(1)}, u32[]{:S(2)}, u32[]{:S(2)}) async-start(bf16[8,1,192,512]{3,0,1,2:T(8,128)(2,1)} %bitcast.208), calls=%async_computation | async-start | bytes 3145728 | tf_op jit(solution)/shard_map/all_to_all | solution.py:69
  89.3 77.1 %all-to-all-start.1 = ((f32[32,8,1,6,512]{4,2,3,1,0:T(1,128)}), f32[32,8,1,6,512]{4,2,3,1,0:T(1,128)S(1)}, u32[]{:S(2)}, u32[]{:S(2)}) async-start(f32[32,8,1,6,512]{4,2,3,1,0:T(1,128)} %fusion.95), calls=%async_computation.1 | async-start | bytes 6291456 | tf_op jit(solution)/shard_map/all_to_all | solution.py:82
  99.0 73.9 %copy-start.3 = (f32[6144]{0:T(1024)S(1)}, f32[6144]{0:T(1024)}, u32[]{:S(2)}) copy-start(f32[6144]{0:T(1024)} %param.9) | copy-start | bytes 73732
  99.0 74.2 %copy-start.5 = (f32[8,64]{1,0:T(8,128)S(1)}, f32[8,64]{1,0:T(8,128)}, u32[]{:S(2)}) copy-start(f32[8,64]{1,0:T(8,128)} %param.7) | copy-start | bytes 6148
  99.0 74.2 %copy-start.4 = (s32[8,64]{1,0:T(8,128)S(1)}, s32[8,64]{1,0:T(8,128)}, u32[]{:S(2)}) copy-start(s32[8,64]{1,0:T(8,128)} %param.8) | copy-start | bytes 6148
  166.4 1.7 copy-start
  168.1 834.5 %all-to-all-start.2 = ((f32[8,32,6,512]{3,0,2,1:T(8,128)}), f32[8,32,6,512]{3,0,2,1:T(8,128)S(1)}, u32[]{:S(2)}, u32[]{:S(2)}) async-start(f32[8,32,6,512]{3,0,2,1:T(8,128)} %copy.43), calls=%async_computation.2 | async-start | bytes 6291456 | tf_op jit(solution)/shard_map/all_to_all | solution.py:85
  172.1 692.9 %all-gather.2.cloned.1.call-start = ((), (), s32[]{:S(2)}) async-start(), calls=%async_computation.4 | async-start | bytes 3158016 | tf_op jit(solution)/shard_map/all_gather | solution.py:42
  172.9 1002.0 %reduce-scatter.4.cloned.1.call-start = ((), (), s32[]{:S(2)}) async-start(), calls=%async_computation.5 | async-start | bytes 270336
  1008.3 5.9 copy-start.2
  1014.3 8.5 copy-start.1
Sparse Core Ops, SparseCore 0:
  174.8 690.1 all-gather.1
  1032.3 142.6 reduce-scatter.3

commit v2 on v0

--- a/solution.py
+++ b/solution.py
@@ -96,9 +96,12 @@
     run_lag = lax.dynamic_slice_in_dim(shifts, mz_rank * run_share, run_share, 0)
     model_re, model_im = own_model(run_amp, run_lag)
     gram_matrix = lax.psum(
-        jnp.einsum("kbr,kbs->rs", weights_col * model_re, model_re, precision=PRECISE)
-        + jnp.einsum("kbr,kbs->rs", weights_col * model_im, model_im, precision=PRECISE),
-        ("freq", "mz"),
+        lax.psum(
+            jnp.einsum("kbr,kbs->rs", weights_col * model_re, model_re, precision=PRECISE)
+            + jnp.einsum("kbr,kbs->rs", weights_col * model_im, model_im, precision=PRECISE),
+            "mz",
+        ),
+        "freq",
     )
     owned = lax.psum_scatter(numerator, "freq", scatter_dimension=1, tiled=True)
     return cholesky_solve(gram_matrix, owned)

time: 1170 us -> 1280 us (1.094)
  blocking collectives: 106 us -> 212 us
    psum x0 -> x1, blocking collectives: none -> 134 us  [on_device(): lax.psum(lax.psum(jnp.einsum('kbr,kbs->rs', weights_col * model_re, model...]
    psum x1, blocking collectives: 106 us -> 78.8 us  [on_device(): lax.psum(jnp.einsum('kbr,kbs->rs', weights_col * model_re, model_re, prec...]
  transfers between devices with their start and end apart: 5 -> 5, of which waited for: 4 -> 4; matrix products, arithmetic and copies ran while one was open for 4% -> 3% of each run, Pallas kernels for 0% -> 0%
where the time goes in v2:
time: 1280 us; the launch traced here: 1270 us
  waiting for transfers between devices  932 us (73%)
  blocking collectives  212 us (17%)
  matrix products  63.8 us (5%)
  starting transfers between devices  17.9 us (1%)
  other arithmetic  14.9 us (1%)
  between operations  14.1 us (1%)
    all_gather x1, waiting for transfers between devices, on_device(): full_elution = lax.all_gather(elution, ('freq', 'mz'), axis=0, tiled=True)  692 us
    psum x1, blocking collectives, on_device(): lax.psum(lax.psum(jnp.einsum('kbr,kbs->rs', weights_col * model_re, model...  134 us
    unnamed x3, waiting for transfers between devices  133 us
    psum x1, blocking collectives, on_device(): lax.psum(jnp.einsum('kbr,kbs->rs', weights_col * model_re, model_re, prec...  78.8 us
    all_to_all x1, waiting for transfers between devices, on_device(): lax.all_to_all(half_re, 'freq', split_axis=1, concat_axis=2, tiled=True)  67.4 us
    all_to_all x1, waiting for transfers between devices, on_device(): lax.all_to_all(intensity.reshape(run_count, 1, bin_count, local_mz), 'fre...  38.9 us
  transfers between devices with their start and end apart: 5, of which 4 were waited for; matrix products, arithmetic and copies ran while one was open for 3% of the time, Pallas kernels for 0%

profile of v2, /device:TPU:8, one launch (start us, length us, event | category | flops | bytes accessed | tf_op | source)
XLA Modules:
  0.0 1267.9 jit_solution(6262598237012247673)
XLA Ops:
  6.5 3.4 copy.76
  10.0 8.7 all-to-all-start
  18.7 0.1 fusion.179
  18.9 38.9 %all-to-all-done = bf16[8,1,192,512]{3,0,1,2:T(8,128)(2,1)S(1)} async-done(((bf16[8,1,192,512]{3,0,1,2:T(8,128)(2,1)}), bf16[8,1,192,512]{3,0,1,2:T(8,128)(2,1)S(1)}, u32[]{:S(2)}, u32[]{:S(2)}) %all-to-all-start) | async-done | bytes 1572896 | tf_op jit(solution)/shard_map/all_to_all | solution.py:69
  57.8 3.0 fusion.14
  60.8 5.3 subtract_bitcast_fusion
  66.1 3.5 copy.42
  69.6 4.3 all-to-all-start.1
  73.9 5.4 copy.44
  79.3 67.4 %all-to-all-done.1 = f32[8,32,6,512]{3,0,2,1:T(8,128)S(1)} async-done(((f32[8,32,6,512]{3,0,2,1:T(8,128)}), f32[8,32,6,512]{3,0,2,1:T(8,128)S(1)}, u32[]{:S(2)}, u32[]{:S(2)}) %all-to-all-start.1) | async-done | bytes 3145760 | tf_op jit(solution)/shard_map/all_to_all | solution.py:81
  146.7 4.8 all-to-all-start.2
  151.5 0.0 all-gather.2.cloned.1.call-start
  151.6 0.7 all-gather.2.cloned.1.call-update
  152.2 0.0 reduce-scatter.4.cloned.1.call-start
  152.3 0.0 copy-done.2
  152.3 0.1 reshape.152
  152.4 0.2 dynamic-slice_reduce_fusion
  152.6 0.0 copy-done.4
  152.6 0.0 copy-done.3
  152.6 0.1 fusion.204
  152.7 0.1 fusion.202
  152.7 692.2 %all-gather.2.cloned.1.call-done = f32[6144,64]{1,0:T(8,128)} async-done(((f32[24,64]{1,0:T(8,128)}), f32[6144,64]{1,0:T(8,128)}) %all-gather.2.cloned.1.call-update) | async-done | bytes 1572880 | tf_op jit(solution)/shard_map/all_gather | solution.py:42
  845.0 2.6 multiply_reduce_fusion
  847.6 1.1 fusion.88
  848.7 1.1 fusion.86
  849.8 1.1 fusion.33
  850.9 1.1 fusion.34
  852.0 0.8 fusion.96
  852.8 0.8 convolution_add_fusion.1
  853.6 78.8 %psum.14 = f32[64,64]{0,1:T(8,128)S(1)} all-reduce(f32[64,64]{0,1:T(8,128)S(1)} %convolution_add_fusion.1), channel_id=1, replica_groups=mesh['freq'=32,'mz'=8] {'mz'}, use_global_device_ids=true, to_apply=%region_0.1 | all-reduce | flops 4096 | bytes 32768 | tf_op jit(solution)/shard_map/psum | solution.py:99
  932.4 133.6 %psum.15 = f32[64,64]{0,1:T(8,128)S(1)} all-reduce(f32[64,64]{0,1:T(8,128)S(1)} %psum.14), channel_id=1, replica_groups=mesh['freq'=32,'mz'=8] {'freq'}, use_global_device_ids=true, to_apply=%region_1.2 | all-reduce | flops 4096 | bytes 32768 | tf_op jit(solution)/shard_map/psum | solution.py:98
  1066.1 0.1 copy.38
  1066.2 5.8 cholesky.16
  1072.0 7.3 fusion.12
  1079.4 7.4 fusion.10
  1086.8 0.0 all-to-all-done.2
  1086.8 7.5 fusion.8
  1094.3 0.0 copy-start.1
  1094.3 7.7 fusion.6
  1102.0 8.6 fusion.18
  1110.6 9.4 fusion.30
  1120.0 0.0 reduce-scatter.4.cloned.1.call-update
  1120.1 0.6 compare_reduce_fusion
  1120.7 0.7 fusion.141
  1121.4 4.9 custom-call.8
  1126.2 132.8 %reduce-scatter.4.cloned.1.call-done = f32[16,64]{1,0:T(8,128)} async-done(((f32[512,64]{1,0:T(8,128)}), f32[16,64]{1,0:T(8,128)}) %reduce-scatter.4.cloned.1.call-update) | async-done | bytes 4112
  1259.0 0.8 fusion.144
  1259.8 0.8 fusion.142
  (12 shorter events, 0.1 us)
Async XLA Ops:
  10.0 47.8 %all-to-all-start = ((bf16[8,1,192,512]{3,0,1,2:T(8,128)(2,1)}), bf16[8,1,192,512]{3,0,1,2:T(8,128)(2,1)S(1)}, u32[]{:S(2)}, u32[]{:S(2)}) async-start(bf16[8,1,192,512]{3,0,1,2:T(8,128)(2,1)} %bitcast.79), calls=%async_computation | async-start | bytes 3145728 | tf_op jit(solution)/shard_map/all_to_all | solution.py:69
  69.6 77.1 %all-to-all-start.1 = ((f32[8,32,6,512]{3,0,2,1:T(8,128)}), f32[8,32,6,512]{3,0,2,1:T(8,128)S(1)}, u32[]{:S(2)}, u32[]{:S(2)}) async-start(f32[8,32,6,512]{3,0,2,1:T(8,128)} %copy.42), calls=%async_computation.1 | async-start | bytes 6291456 | tf_op jit(solution)/shard_map/all_to_all | solution.py:81
  79.3 73.0 %copy-start.2 = (f32[6144]{0:T(1024)S(1)}, f32[6144]{0:T(1024)}, u32[]{:S(2)}) copy-start(f32[6144]{0:T(1024)} %param.9) | copy-start | bytes 73732
  79.3 73.3 %copy-start.4 = (f32[8,64]{1,0:T(8,128)S(1)}, f32[8,64]{1,0:T(8,128)}, u32[]{:S(2)}) copy-start(f32[8,64]{1,0:T(8,128)} %param.7) | copy-start | bytes 6148
  79.3 73.3 %copy-start.3 = (s32[8,64]{1,0:T(8,128)S(1)}, s32[8,64]{1,0:T(8,128)}, u32[]{:S(2)}) copy-start(s32[8,64]{1,0:T(8,128)} %param.8) | copy-start | bytes 6148
  146.7 940.1 %all-to-all-start.2 = ((f32[8,32,6,512]{3,0,2,1:T(8,128)}), f32[8,32,6,512]{3,0,2,1:T(8,128)}, u32[]{:S(2)}, u32[]{:S(2)}) async-start(f32[8,32,6,512]{3,0,2,1:T(8,128)} %copy.44), calls=%async_computation.2 | async-start | bytes 6291456 | tf_op jit(solution)/shard_map/all_to_all | solution.py:82
  151.5 693.4 %all-gather.2.cloned.1.call-start = ((), (), s32[]{:S(2)}) async-start(), calls=%async_computation.4 | async-start | bytes 3158016 | tf_op jit(solution)/shard_map/all_gather | solution.py:42
  152.2 1106.8 %reduce-scatter.4.cloned.1.call-start = ((), (), s32[]{:S(2)}) async-start(), calls=%async_computation.5 | async-start | bytes 270336
  1094.3 7.7 copy-start.1
  1102.0 8.7 copy-start
Sparse Core Ops, SparseCore 0:
  154.2 690.7 all-gather.1
  1120.2 138.7 reduce-scatter.3
